TPU v7x, 32 devices: a whole 2x2x4 slice. The times are simulated.
32 devices in a mesh: grid: 8 (over z, y), vis: 4 (over x, core).
Axes of the slice: x: 2, y: 2, z: 4, core: 2. Of those that a mesh axis runs over, the one named last changes fastest.
Arguments:
- vis_coords: float32 [8, 256, 2, 512], P('grid', 'vis'), may hold values from 0 to 64
- vis_values: float32 [8, 256, 2, 512], P('grid', 'vis'), may hold values from -6 to 6
- tile_index: int32 [8, 256], P('grid', 'vis'), may hold values from 0 to 63
Outputs:
- facets: float32 [8, 2, 1024, 1024], P('grid', None, 'vis')
Inputs may be any that keep to these rules, and one draw needn't show every extreme that they name: `tile_index`: tile a * 8 + e covers subgrid rows from a * 64 and columns from e * 64.
All inputs are finite; a program needn't handle non-finite values.
Results may differ from a plain program's by a relative error of at most 0.014.
Values may be sent and summed in bfloat16 or wider, within the bound.
A program may use at most 64 MiB of HBM per device.

v0:
```python
import math

import jax
import jax.numpy as jnp
from jax import lax
from jax.sharding import PartitionSpec as P

SUB = 512
FAC = 1024
CONTRIB = 64
TILE = 64
NBLK = 8


taper_scale = 16.0


def phase_pair(frequencies, points, length):
    phases = frequencies[:, None] * points[None, :] % length
    angles = phases.astype(jnp.float32) * (2.0 * math.pi / length)
    return (jnp.cos(angles), jnp.sin(angles))


def kernel_rows(places):
    pixels = jnp.arange(TILE, dtype=jnp.float32)
    distance = pixels - places[..., None]
    scaled = distance / taper_scale
    return jnp.sinc(distance) * jnp.exp(-scaled * scaled)


def complex_block(part_real, part_imag):
    return jnp.concatenate(
        [jnp.concatenate([part_real, part_imag], 1), jnp.concatenate([-part_imag, part_real], 1)], 0
    )


def shards(vis_coords, vis_values, tile_index):
    coords = vis_coords[0]
    values = vis_values[0]
    tile_ids = tile_index[0]
    blocks_here = coords.shape[0]
    across = SUB // TILE
    grid_count = lax.axis_size("grid")
    vis_count = lax.axis_size("vis")
    vis_index = lax.axis_index("vis")
    groups = grid_count // NBLK
    column_count = groups * CONTRIB
    quarter = CONTRIB // vis_count
    rows_here = FAC // vis_count
    unitary = 1.0 / math.sqrt(SUB)
    weights_u = kernel_rows(coords[:, 0])
    weights_v = kernel_rows(coords[:, 1])
    weighted = weights_u[:, None] * values[:, :, :, None]
    patches = jnp.einsum(
        "bcnx,bny->bcxy",
        weighted,
        weights_v,
        precision=lax.Precision.HIGHEST,
        preferred_element_type=jnp.float32,
    )
    onehot = (tile_ids[None, :] == jnp.arange(across * across, dtype=jnp.int32)[:, None]).astype(
        jnp.float32
    )
    placed = jnp.dot(
        onehot,
        patches.reshape(blocks_here, 2 * TILE * TILE),
        precision=lax.Precision.HIGHEST,
        preferred_element_type=jnp.float32,
    )
    placed = (
        placed.reshape(across, across, 2, TILE, TILE).transpose(0, 3, 2, 1, 4).reshape(SUB, 2, SUB)
    )
    rounded = lax.optimization_barrier(placed.astype(jnp.bfloat16)).astype(jnp.float32)
    spectrum = jnp.arange(SUB, dtype=jnp.int32)
    tab_real, tab_imag = phase_pair(spectrum, jnp.arange(column_count, dtype=jnp.int32), SUB)
    col_table = jnp.concatenate(
        [jnp.concatenate([tab_real, -tab_imag], 1), jnp.concatenate([tab_imag, tab_real], 1)], 0
    ).astype(jnp.bfloat16)
    picked = (
        jnp.arange(NBLK, dtype=jnp.int32)[:, None] * CONTRIB
        + vis_index * quarter
        + jnp.arange(quarter, dtype=jnp.int32)[None, :]
    ).reshape(NBLK * quarter)
    rows_real, rows_imag = phase_pair(picked, spectrum, SUB)
    rows_real = rows_real.astype(jnp.bfloat16)
    rows_neg = (-rows_imag).astype(jnp.bfloat16)
    summed = lax.psum_scatter(rounded.astype(jnp.bfloat16), "vis", scatter_dimension=0, tiled=True)
    height = summed.shape[0]
    result = (
        jnp.dot(summed.reshape(height, 2 * SUB), col_table, preferred_element_type=jnp.float32)
        * unitary
    )
    images = result.astype(jnp.bfloat16).reshape(height, 2, column_count)
    portion = lax.all_gather(images, "vis", axis=0, tiled=True)
    stacked = complex_block(portion[:, 0], portion[:, 1])
    left_side = jnp.concatenate([rows_real, rows_neg], 1)
    spectra = jnp.dot(left_side, stacked, preferred_element_type=jnp.float32)
    spectra = (spectra * unitary).astype(jnp.bfloat16)
    outgoing = (
        spectra.reshape(NBLK, quarter, 2, groups, CONTRIB)
        .transpose(3, 0, 2, 1, 4)
        .reshape(grid_count, 2 * quarter * CONTRIB)
    )
    arrived = lax.all_to_all(outgoing, "grid", split_axis=0, concat_axis=0, tiled=True)
    arrived = arrived.reshape(grid_count, 2, quarter, CONTRIB)
    row_ids = vis_index * rows_here + jnp.arange(rows_here, dtype=jnp.int32)
    embed_real, embed_imag = phase_pair(row_ids, spectrum, FAC)
    embed_real = embed_real.astype(jnp.bfloat16).reshape(rows_here, NBLK, CONTRIB)
    embed_imag = embed_imag.astype(jnp.bfloat16).reshape(rows_here, NBLK, CONTRIB)
    portion = lax.all_gather(arrived, "vis", axis=2, tiled=True)
    extent = portion.shape[2]
    blocks = portion.reshape(groups, NBLK, 2, extent, CONTRIB).transpose(1, 3, 2, 0, 4)
    part_real = blocks[:, :, 0].reshape(NBLK * extent, column_count)
    part_imag = blocks[:, :, 1].reshape(NBLK * extent, column_count)
    left_real = embed_real.reshape(rows_here, NBLK * extent)
    left_imag = embed_imag.reshape(rows_here, NBLK * extent)
    left_side = jnp.concatenate([left_real, left_imag], 1)
    mixture = jnp.dot(
        left_side, complex_block(part_real, part_imag), preferred_element_type=jnp.float32
    )
    mixture = (mixture * unitary).astype(jnp.bfloat16)
    out_real, out_imag = phase_pair(
        jnp.arange(column_count, dtype=jnp.int32), jnp.arange(FAC, dtype=jnp.int32), FAC
    )
    real_right = jnp.concatenate([out_real, -out_imag], 0).astype(jnp.bfloat16)
    imag_right = jnp.concatenate([out_imag, out_real], 0).astype(jnp.bfloat16)
    row_sines = jnp.sin(math.pi * (row_ids.astype(jnp.float32) + 0.5) / FAC)
    col_sines = jnp.sin(math.pi * (jnp.arange(FAC, dtype=jnp.float32) + 0.5) / FAC)
    taper_rows = 0.25 + 0.75 * row_sines * row_sines
    taper_cols = 0.25 + 0.75 * col_sines * col_sines
    weight = taper_rows[:, None] * taper_cols[None, :] * (1.0 / math.sqrt(CONTRIB * groups))
    image_real = jnp.dot(mixture, real_right, preferred_element_type=jnp.float32) * weight
    image_imag = jnp.dot(mixture, imag_right, preferred_element_type=jnp.float32) * weight
    return jnp.stack([image_real, image_imag])[None]


def solution(mesh):
    placed = (P("grid", "vis", None, None), P("grid", "vis", None, None), P("grid", "vis"))
    return jax.shard_map(
        shards, mesh=mesh, in_specs=placed, out_specs=P("grid", None, "vis", None), check_vma=False
    )
```

profile of v0, /device:TPU:0, one launch (start us, length us, event | category | flops | bytes accessed | tf_op | source)
XLA Modules:
  0.0 128.6 jit_solution(8931547800467596844)
XLA Ops:
  6.5 1.3 %fusion.138 = (f32[64,1,512]{2,1,0:T(1,128)S(1)}, f32[64,1,512]{2,1,0:T(1,128)S(1)}) fusion(f32[64,2,512]{2,1,0:T(2,128)} %bitcast.60), kind=kLoop, calls=%fused_computation.200 | loop fusion | bytes 524288 | tf_op jit(solution)/shard_map/slice | solution.py:52
  7.9 11.1 %fusion.11 = f32[64,512,64]{1,2,0:T(8,128)S(1)} fusion(f32[64,512]{1,0:T(8,128)S(1)} %get-tuple-element.17), kind=kLoop, calls=%fused_computation.25 | loop fusion | flops 79691776 | bytes 8519680 | tf_op jit(solution)/shard_map/mul | solution.py:28
  19.0 27.9 %fusion = f32[64,2,64,64]{3,2,1,0:T(8,128)} fusion(f32[64,2,512]{2,1,0:T(2,128)S(1)} %bitcast.66, f32[64,512,64]{1,2,0:T(8,128)S(1)} %fusion.11, f32[64,512]{1,0:T(8,128)S(1)} %get-tuple-element.16), kind=kOutput, calls=%fused_computation | convolution fusion | flops 3305111552 | bytes 10878976 | tf_op jit(solution)/shard_map/bcnx,bny->bcxy/dot_general | solution.py:54
  46.9 3.5 %reshape.92 = f32[64,8192]{1,0:T(8,128)S(1)} reshape(f32[64,2,64,64]{3,2,1,0:T(8,128)} %fusion) | data formatting | bytes 4194304 | tf_op jit(solution)/shard_map/reshape | solution.py:66
  50.5 2.7 %copy.17 = f32[8192,64]{1,0:T(8,128)} copy(f32[8192,64]{0,1:T(8,128)S(1)} %bitcast.57) | data formatting | bytes 4194304 | tf_op jit(solution)/shard_map/dot_general | solution.py:64
  53.2 8.3 %convert_bitcast_fusion = bf16[8,64,2,8,64]{4,3,1,2,0:T(8,128)(2,1)S(1)} fusion(f32[2,64,64,64,1]{3,2,1,0,4:T(8,128)} %bitcast.56, s32[8,8]{1,0:T(8,128)S(1)} %multiply_add_fusion.2, s32[64]{0:T(128)S(1)} %bitcast.65), kind=kOutput, calls=%fused_computation.71 | convolution fusion | flops 403181568 | bytes 3146240 | tf_op jit(solution)/shard_map/dot_general | solution.py:64
  61.6 2.0 %convert_element_type.78 = bf16[512,2,512]{2,0,1:T(8,128)(2,1)} reshape(bf16[8,64,2,8,64]{4,3,1,0,2:T(8,128)(2,1)S(1)} %copy.18) | data formatting | bytes 2097152 | tf_op jit(solution)/shard_map/convert_element_type | solution.py:73
  63.9 1.0 fusion.112
  64.9 1.0 negate_convert_fusion
  65.9 1.1 negate_convert_fusion.1
  67.0 1.1 cosine_convert_fusion.1
  68.1 1.2 cosine_convert_fusion.3
  69.4 2.5 %cosine_convert_fusion = (bf16[256,512]{1,0:T(8,128)(2,1)S(1)}, bf16[256,512]{1,0:T(8,128)(2,1)S(1)}) fusion(s32[256]{0:T(256)S(1)} %iota_add_fusion.1), kind=kLoop, calls=%fused_computation.93 | loop fusion | flops 2097152 | bytes 525312 | tf_op jit(solution)/shard_map/convert_element_type | solution.py:108
  71.8 19.5 %reduce-scatter.2.cloned.1.call-done = bf16[128,2,512]{2,0,1:T(8,128)(2,1)} async-done(((bf16[512,2,512]{2,0,1:T(8,128)(2,1)}), bf16[128,2,512]{2,0,1:T(8,128)(2,1)}) %reduce-scatter.2.cloned.1.call-update) | async-done | bytes 262160 | tf_op jit(solution)/shard_map/reduce_scatter | solution.py:87
  91.4 1.1 copy.19
  92.9 5.4 %all_gather.6 = bf16[512,2,64]{0,2,1:T(8,128)(2,1)S(1)} all-gather(bf16[128,2,64]{0,2,1:T(8,128)(2,1)S(1)} %bitcast.64), channel_id=1, replica_groups=mesh['grid'=8,'vis'=4] {'vis'}, dimensions={0}, use_global_device_ids=true | all-gather | bytes 163840 | tf_op jit(solution)/shard_map/all_gather | solution.py:94
  98.9 0.5 broadcast.168
  99.5 0.8 reduce.1
  100.3 0.6 reshape.102
  100.9 5.5 %all-to-all-start = ((bf16[8,2,1024]{2,1,0:T(2,128)(2,1)}), bf16[8,2,1024]{2,1,0:T(2,128)(2,1)S(1)}, u32[]{:S(2)}, u32[]{:S(2)}) async-start(bf16[8,2,1024]{2,1,0:T(2,128)(2,1)} %reshape.102), calls=%async_computation.1 | async-start | bytes 65536 | tf_op jit(solution)/shard_map/all_to_all | solution.py:104
  106.5 6.6 %all-to-all-done = bf16[8,2,1024]{2,1,0:T(2,128)(2,1)S(1)} async-done(((bf16[8,2,1024]{2,1,0:T(2,128)(2,1)}), bf16[8,2,1024]{2,1,0:T(2,128)(2,1)S(1)}, u32[]{:S(2)}, u32[]{:S(2)}) %all-to-all-start) | async-done | bytes 32800 | tf_op jit(solution)/shard_map/all_to_all | solution.py:104
  113.4 5.8 %all_gather.7 = bf16[8,2,64,64]{3,2,1,0:T(8,128)(2,1)S(1)} all-gather(bf16[8,2,16,64]{3,2,1,0:T(8,128)(2,1)S(1)} %reshape.96), channel_id=1, replica_groups=mesh['grid'=8,'vis'=4] {'vis'}, dimensions={2}, use_global_device_ids=true | all-gather | bytes 163840 | tf_op jit(solution)/shard_map/all_gather | solution.py:110
  119.3 0.4 fusion.49
  120.3 1.5 %maximum_bitcast_fusion = f32[1,2,256,1024]{3,2,1,0:T(8,128)} fusion(f32[1,256,1024]{2,1,0:T(8,128)S(1)} %fusion.47, f32[1,256,1024]{2,1,0:T(8,128)S(1)} %fusion.48), kind=kLoop, calls=%fused_computation.70 | loop fusion | flops 524288 | bytes 4194304 | tf_op jit(solution)/shard_map/broadcast_in_dim | solution.py:134
  (30 shorter events, 2.4 us)
Async XLA Ops:
  6.5 12.5 %copy-start.1 = (f32[1,64,2,512]{3,2,1,0:T(2,128)S(1)}, f32[1,64,2,512]{3,2,1,0:T(2,128)}, u32[]{:S(2)}) copy-start(f32[1,64,2,512]{3,2,1,0:T(2,128)} %param.5) | copy-start | bytes 786436
  6.5 84.8 %reduce-scatter.2.cloned.1.call-start = ((), (), s32[]{:S(2)}) async-start(), calls=%async_computation.2 | async-start | bytes 1310720 | tf_op jit(solution)/shard_map/reduce_scatter | solution.py:87
  46.9 6.3 %copy-start = (s32[1,64]{1,0:T(1,128)S(1)}, s32[1,64]{1,0:T(1,128)}, u32[]{:S(2)}) copy-start(s32[1,64]{1,0:T(1,128)} %param.6) | copy-start | bytes 772
  100.9 12.2 %all-to-all-start = ((bf16[8,2,1024]{2,1,0:T(2,128)(2,1)}), bf16[8,2,1024]{2,1,0:T(2,128)(2,1)S(1)}, u32[]{:S(2)}, u32[]{:S(2)}) async-start(bf16[8,2,1024]{2,1,0:T(2,128)(2,1)} %reshape.102), calls=%async_computation.1 | async-start | bytes 65536 | tf_op jit(solution)/shard_map/all_to_all | solution.py:104
Sparse Core Ops, SparseCore 0:
  63.8 27.4 reduce-scatter.1
where the time goes:
time: 129 us
  matrix products  37.8 us (29%)
  waiting for transfers between devices  26.2 us (20%)
  other arithmetic  21.7 us (17%)
  between operations  13.6 us (11%)
  local copies, waits for them, and re-layouts  12.6 us (10%)
  blocking collectives  11.2 us (9%)
  starting transfers between devices  5.49 us (4%)
    dot_general x1, matrix products, shards(): jnp.einsum('bcnx,bny->bcxy', weighted, weights_v, precision=lax.Precision...  27.9 us
    reduce_scatter x1, waiting for transfers between devices, shards(): lax.psum_scatter(rounded.astype(jnp.bfloat16), 'vis', scatter_dimension=0...  19.5 us
    mul x1, other arithmetic, kernel_rows(): return jnp.sinc(distance) * jnp.exp(-scaled * scaled)  11.1 us
    dot_general x1, matrix products, shards(): jnp.dot(onehot, patches.reshape(blocks_here, 2 * TILE * TILE), precision=...  8.31 us
    all_to_all x1, waiting for transfers between devices, shards(): lax.all_to_all(outgoing, 'grid', split_axis=0, concat_axis=0, tiled=True)  6.64 us
    all_gather x1, blocking collectives, shards(): portion = lax.all_gather(arrived, 'vis', axis=2, tiled=True)  5.78 us
    all_to_all x1, starting transfers between devices, shards(): lax.all_to_all(outgoing, 'grid', split_axis=0, concat_axis=0, tiled=True)  5.49 us
    all_gather x1, blocking collectives, shards(): portion = lax.all_gather(images, 'vis', axis=0, tiled=True)  5.45 us
  transfers between devices with their start and end apart: 2, of which 2 were waited for; matrix products, arithmetic and copies ran while one was open for 6% of the time, Pallas kernels for 0%

commit v1 on v0

v1 whole, which is shorter than its diff:
```python
import functools
import math

import jax
import jax.numpy as jnp
import ml_dtypes
import numpy as np
from jax import lax
from jax.experimental import pallas as pl
from jax.experimental.pallas import tpu as pltpu
from jax.sharding import PartitionSpec as P

SUB = 512
FAC = 1024
CONTRIB = 64
TILE = 64
NBLK = 8
LANES = 2 * CONTRIB
TAPER_SCALE = 16.0
MESH = pl.DeviceIdType.MESH


def phase_pair(frequencies, points, length):
    phases = (frequencies[:, None] * points[None, :]) % length
    angles = phases * (2.0 * math.pi / length)
    return np.cos(angles).astype(np.float32), np.sin(angles).astype(np.float32)


def as_bf16(array):
    return array.astype(ml_dtypes.bfloat16)


def column_table(groups):
    cos, sin = phase_pair(np.arange(SUB), np.arange(groups * CONTRIB), SUB)
    across = SUB // TILE
    table = np.zeros((across, 2, TILE, groups, 4, CONTRIB), np.float32)
    cos = cos.reshape(across, TILE, groups, CONTRIB)
    sin = sin.reshape(across, TILE, groups, CONTRIB)
    table[:, 0, :, :, 0], table[:, 1, :, :, 0] = cos, sin
    table[:, 0, :, :, 1], table[:, 1, :, :, 1] = -sin, cos
    table[:, :, :, :, 2] = -table[:, :, :, :, 1]
    table[:, :, :, :, 3] = table[:, :, :, :, 0]
    return as_bf16(table.reshape(2 * SUB, groups * 4 * CONTRIB))


def row_table(vis_count):
    quarter = CONTRIB // vis_count
    order = np.arange(SUB).reshape(NBLK, vis_count, quarter).transpose(1, 0, 2).reshape(SUB)
    cos, sin = phase_pair(order, np.arange(SUB), SUB)
    return as_bf16(np.concatenate([cos, -sin], 1))


def embed_table():
    cos, sin = phase_pair(np.arange(FAC), np.arange(SUB), FAC)
    return as_bf16(np.concatenate([cos, sin], 1))


def output_table(groups):
    cos, sin = phase_pair(np.arange(groups * CONTRIB), np.arange(FAC), FAC)
    cos = cos.reshape(groups, CONTRIB, FAC)
    sin = sin.reshape(groups, CONTRIB, FAC)
    real = np.stack([cos, -sin], 1).reshape(groups * LANES, FAC)
    imag = np.stack([sin, cos], 1).reshape(groups * LANES, FAC)
    return as_bf16(np.concatenate([real, imag], 1))


def taper():
    sines = np.sin(np.pi * (np.arange(FAC) + 0.5) / FAC)
    return 0.25 + 0.75 * sines * sines


SINE = [(-1.0) ** k * math.pi ** (2 * k) / math.factorial(2 * k + 1) for k in range(7)]


def grid_kernel(tiles, coords, values, out, total):
    blocks = coords.shape[0]
    total[...] = jnp.zeros_like(total)
    pixel = lax.broadcasted_iota(jnp.int32, (TILE, 1), 0)
    place = pixel.astype(jnp.float32)
    flip = 1.0 - 2.0 * (pixel % 2).astype(jnp.float32)

    def block(b, carry):
        where = coords[b]
        nearest = jnp.floor(where + 0.5)
        offset = where - nearest
        offset = jnp.where(offset == 0.0, 1e-30, offset)
        square = offset * offset
        wave = jnp.full_like(square, SINE[6])
        for k in range(5, -1, -1):
            wave = wave * square + SINE[k]
        half = nearest * 0.5
        odd = (half - jnp.floor(half)) * 4.0 - 1.0
        wave = wave * offset * odd

        def rows(axis):
            distance = (place - nearest[axis : axis + 1]) - offset[axis : axis + 1]
            near = pl.reciprocal(distance, approx=True)
            near = near * (2.0 - distance * near)
            fall = jnp.exp(distance * distance * (-1.0 / (TAPER_SCALE * TAPER_SCALE)))
            return (flip * wave[axis : axis + 1]) * fall * near

        along = rows(0).astype(jnp.bfloat16)
        down = rows(1)
        data = values[b]
        right = jnp.concatenate([down * data[0:1], down * data[1:2]], 0).astype(jnp.bfloat16)
        patch = lax.dot_general(
            along, right, (((1,), (1,)), ((), ())), preferred_element_type=jnp.float32
        )
        tile = tiles[0, b]
        r = pl.ds(pl.multiple_of(tile // (SUB // TILE) * TILE, TILE), TILE)
        c = pl.ds(pl.multiple_of(tile % (SUB // TILE) * (2 * TILE), 2 * TILE), 2 * TILE)
        total[r, c] += patch
        return carry

    lax.fori_loop(0, blocks, block, 0, unroll=4)
    out[...] = total[...].astype(jnp.bfloat16)


def swapped(index, bits):
    result = index
    bit = 1
    while bit <= bits:
        if bits & bit:
            result = result + bit * (1 - 2 * ((index // bit) % 2))
        bit *= 2
    return result


def exchange_kernel(
    grid_count, vis_count, unitary, part_hbm, col_hbm, row_hbm, embed_hbm, scale_hbm, out,
    part, col, row, embed, scale, spectra, pieces, summed, gathered,
    load_sem, send1, recv1, send2, recv2, send3, recv3,
):
    me_g, me_v = lax.axis_index("grid"), lax.axis_index("vis")
    groups = grid_count // NBLK
    rows_here = out.shape[0]
    quarter = CONTRIB // vis_count
    peers_v = [lax.rem(me_v + k, vis_count) for k in range(vis_count)]
    peers_g = [swapped(me_g, k) for k in range(grid_count)]
    mine = pl.ds(pl.multiple_of(me_v * rows_here, rows_here), rows_here)
    loads = [
        pltpu.make_async_copy(src, dst, load_sem.at[i])
        for i, (src, dst) in enumerate(
            [(part_hbm, part), (col_hbm, col), (row_hbm, row),
             (embed_hbm.at[mine], embed), (scale_hbm.at[mine], scale)]
        )
    ]
    for load in loads:
        load.start()
    barrier = pltpu.get_barrier_semaphore()
    for k in range(grid_count - 1, 0, -1):
        pl.semaphore_signal(barrier, inc=1, device_id=(peers_g[k], me_v), device_id_type=MESH)
    for k in range(1, vis_count):
        pl.semaphore_signal(barrier, inc=1, device_id=(me_g, peers_v[k]), device_id_type=MESH)

    loads[0].wait()
    loads[1].wait()
    loads[2].wait()
    for g in range(groups):
        image = jnp.dot(
            part[...], col[:, 2 * LANES * g : 2 * LANES * (g + 1)], preferred_element_type=jnp.float32
        )
        image = (image * unitary).astype(jnp.bfloat16)
        both = jnp.concatenate([image[:, :LANES], image[:, LANES:]], 0)
        result = jnp.dot(row[...], both, preferred_element_type=jnp.float32)
        result = (result * unitary).astype(jnp.bfloat16)
        spectra[:, NBLK * g : NBLK * (g + 1)] = result.reshape(vis_count, NBLK, quarter, LANES)

    pl.semaphore_wait(barrier, grid_count + vis_count - 2)

    def copy1(k):
        return pltpu.make_async_remote_copy(
            src_ref=spectra.at[peers_v[k]], dst_ref=pieces.at[k], send_sem=send1.at[k],
            recv_sem=recv1.at[k], device_id=(me_g, peers_v[k]), device_id_type=MESH,
        )

    def copy2(k):
        return pltpu.make_async_remote_copy(
            src_ref=summed.at[peers_g[k]], dst_ref=gathered.at[me_g, me_v], send_sem=send2.at[k],
            recv_sem=recv2.at[k], device_id=(peers_g[k], me_v), device_id_type=MESH,
        )

    def copy3(k, j):
        spot = gathered.at[peers_g[k], me_v]
        return pltpu.make_async_remote_copy(
            src_ref=spot, dst_ref=spot, send_sem=send3.at[k, j],
            recv_sem=recv3.at[k, j], device_id=(me_g, peers_v[j]), device_id_type=MESH,
        )

    for k in range(1, vis_count):
        copy1(k).start()
    whole = spectra[me_v].astype(jnp.float32)
    for k in range(1, vis_count):
        copy1(k).wait_recv()
        whole = whole + pieces[k].astype(jnp.float32)
    summed[...] = whole.astype(jnp.bfloat16)
    for k in range(grid_count - 1, 0, -1):
        copy2(k).start()
    gathered[me_g, me_v] = summed[me_g]
    for k in range(grid_count):
        if k > 0:
            copy2(k).wait_recv()
        for j in range(1, vis_count):
            copy3(k, j).start()
    loads[3].wait()
    loads[4].wait()
    for k in range(grid_count):
        for j in range(1, vis_count):
            copy3(k, j).wait_recv()
    sign = jnp.where(lax.broadcasted_iota(jnp.int32, (1, LANES), 1) < CONTRIB, -1.0, 1.0)
    for g in range(groups):
        straight = gathered[NBLK * g : NBLK * (g + 1)].reshape(SUB, LANES)
        turned = pltpu.roll(straight.astype(jnp.float32), CONTRIB, 1) * sign
        both = jnp.concatenate([straight, turned.astype(jnp.bfloat16)], 0)
        mixture = jnp.dot(embed[...], both, preferred_element_type=jnp.float32)
        out[:, LANES * g : LANES * (g + 1)] = (mixture * scale[...]).astype(jnp.bfloat16)
    for k in range(1, vis_count):
        copy1(k).wait_send()
    for k in range(1, grid_count):
        copy2(k).wait_send()
    for k in range(grid_count):
        for j in range(1, vis_count):
            copy3(k, j).wait_send()


def image_kernel(mixture, table, weight, out):
    result = jnp.dot(mixture[...], table[...], preferred_element_type=jnp.float32)
    out[0, 0] = result * weight[...]


def shards(grid_count, vis_count, vis_coords, vis_values, tile_index):
    groups = grid_count // NBLK
    quarter = CONTRIB // vis_count
    rows_here = FAC // vis_count
    unitary = 1.0 / math.sqrt(SUB)
    bf16, f32 = jnp.bfloat16, jnp.float32
    blocks = vis_coords.shape[1]
    visible = vis_coords.shape[3]
    partial = pl.pallas_call(
        grid_kernel,
        out_shape=jax.ShapeDtypeStruct((SUB, 2 * SUB), bf16),
        in_specs=[
            pl.BlockSpec(memory_space=pltpu.SMEM),
            pl.BlockSpec(memory_space=pltpu.VMEM),
            pl.BlockSpec(memory_space=pltpu.VMEM),
        ],
        out_specs=pl.BlockSpec(memory_space=pltpu.VMEM),
        scratch_shapes=[pltpu.VMEM((SUB, 2 * SUB), f32)],
        name="gridding",
    )(tile_index, vis_coords.reshape(blocks, 2, visible), vis_values.reshape(blocks, 2, visible))

    row_scale = taper() * (unitary / math.sqrt(CONTRIB * groups))
    row_scale = np.broadcast_to(row_scale[:, None], (FAC, LANES)).astype(np.float32)
    any_spec = pl.BlockSpec(memory_space=pl.ANY)
    dma = pltpu.SemaphoreType.DMA
    mixture = pl.pallas_call(
        functools.partial(exchange_kernel, grid_count, vis_count, unitary),
        out_shape=jax.ShapeDtypeStruct((rows_here, groups * LANES), bf16),
        in_specs=[any_spec] * 5,
        out_specs=pl.BlockSpec(memory_space=pltpu.VMEM),
        scratch_shapes=[
            pltpu.VMEM((SUB, 2 * SUB), bf16),
            pltpu.VMEM((2 * SUB, groups * 2 * LANES), bf16),
            pltpu.VMEM((SUB, 2 * SUB), bf16),
            pltpu.VMEM((rows_here, 2 * SUB), bf16),
            pltpu.VMEM((rows_here, LANES), f32),
            pltpu.VMEM((vis_count, grid_count, quarter, LANES), bf16),
            pltpu.VMEM((vis_count, grid_count, quarter, LANES), bf16),
            pltpu.VMEM((grid_count, quarter, LANES), bf16),
            pltpu.VMEM((grid_count, vis_count, quarter, LANES), bf16),
            dma((5,)),
            dma((vis_count,)),
            dma((vis_count,)),
            dma((grid_count,)),
            dma((grid_count,)),
            dma((grid_count, vis_count)),
            dma((grid_count, vis_count)),
        ],
        compiler_params=pltpu.CompilerParams(collective_id=0, has_side_effects=True),
        name="exchange",
    )(
        partial,
        jnp.asarray(column_table(groups)),
        jnp.asarray(row_table(vis_count)),
        jnp.asarray(embed_table()),
        jnp.asarray(row_scale),
    )

    halves = 2
    wide = FAC // halves
    return pl.pallas_call(
        image_kernel,
        grid=(2, halves),
        out_shape=jax.ShapeDtypeStruct((1, 2, rows_here, FAC), f32),
        in_specs=[
            pl.BlockSpec((rows_here, groups * LANES), lambda c, h: (0, 0)),
            pl.BlockSpec((groups * LANES, wide), lambda c, h: (0, c * halves + h)),
            pl.BlockSpec((1, wide), lambda c, h: (0, h)),
        ],
        out_specs=pl.BlockSpec((1, 1, rows_here, wide), lambda c, h: (0, c, 0, h)),
        name="images",
    )(
        mixture,
        jnp.asarray(output_table(groups)),
        jnp.asarray(taper()[None, :].astype(np.float32)),
    )


def solution(mesh):
    placed = (P("grid", "vis", None, None), P("grid", "vis", None, None), P("grid", "vis"))
    body = functools.partial(shards, mesh.shape["grid"], mesh.shape["vis"])
    return jax.shard_map(
        body, mesh=mesh, in_specs=placed, out_specs=P("grid", None, "vis", None), check_vma=False
    )
```

time: 129 us -> 35 us (0.27)
  matrix products: 37.8 us -> 0 us
  Pallas kernels: 0 us -> 34.8 us
  waiting for transfers between devices: 26.2 us -> 0 us
  other arithmetic: 21.7 us -> 0 us
  between operations: 13.6 us -> 0.01 us
  local copies, waits for them, and re-layouts: 12.6 us -> 0 us
  blocking collectives: 11.2 us -> 0 us
  starting transfers between devices: 5.49 us -> 0 us
    dot_general x7 -> x0, matrix products: 37.8 us -> none  [the longest x1 27.9 us: shards(): jnp.einsum('bcnx,bny->bcxy', weighted, weights_v, precision=lax.Precision...]
    pallas_call x0 -> x3, Pallas kernels: none -> 34.8 us  [the longest x1 17.9 us: shards(): pl.pallas_call(functools.partial(exchange_kernel, grid_count, vis_count,...]
    reduce_scatter x1 -> x0, waiting for transfers between devices: 19.5 us -> none  [shards(): lax.psum_scatter(rounded.astype(jnp.bfloat16), 'vis', scatter_dimension=0...]
    all_gather x2 -> x0, blocking collectives: 11.2 us -> none  [the longest x1 5.78 us: shards(): portion = lax.all_gather(arrived, 'vis', axis=2, tiled=True)]
    mul x1 -> x0, other arithmetic: 11.1 us -> none  [kernel_rows(): return jnp.sinc(distance) * jnp.exp(-scaled * scaled)]
    all_to_all x1 -> x0, waiting for transfers between devices: 6.64 us -> none  [shards(): lax.all_to_all(outgoing, 'grid', split_axis=0, concat_axis=0, tiled=True)]
    all_to_all x1 -> x0, starting transfers between devices: 5.49 us -> none  [shards(): lax.all_to_all(outgoing, 'grid', split_axis=0, concat_axis=0, tiled=True)]
    another operation x4 -> x0, other arithmetic: 4.15 us -> none
  transfers between devices with their start and end apart: 2 -> 0, of which waited for: 2 -> 0; matrix products, arithmetic and copies ran while one was open for 6% -> 0% of each run, Pallas kernels for 0% -> 0%
where the time goes in v1:
time: 35 us; the launch traced here: 34.8 us
  Pallas kernels  34.8 us (99%)
    pallas_call x1, Pallas kernels, shards(): pl.pallas_call(functools.partial(exchange_kernel, grid_count, vis_count,...  17.9 us
    pallas_call x1, Pallas kernels, shards(): pl.pallas_call(grid_kernel, out_shape=jax.ShapeDtypeStruct((SUB, 2 * SUB)...  13 us
    pallas_call x1, Pallas kernels, shards(): pl.pallas_call(image_kernel, grid=(2, halves), out_shape=jax.ShapeDtypeSt...  3.88 us

profile of v1, /device:TPU:0, one launch (start us, length us, event | category | flops | bytes accessed | tf_op | source)
XLA Modules:
  0.0 34.8 jit_solution(4128812041751158756)
XLA Ops:
  0.0 13.0 %gridding.1.part_hbm = bf16[512,1024]{1,0:T(8,128)(2,1)} custom-call(s32[1,64]{1,0:T(1,128)} %tiles.1, f32[64,2,512]{2,1,0:T(2,128)} %bitcast.2, f32[64,2,512]{2,1,0:T(2,128)} %bitcast.3), custom_call_target="tpu_custom_call" | custom-call | tf_op jit(solution)/shard_map/gridding/pallas_call | solution.py:239
  13.0 17.9 %exchange.1.mixture = bf16[256,128]{1,0:T(8,128)(2,1)} custom-call(bf16[512,1024]{1,0:T(8,128)(2,1)} %gridding.1.part_hbm, bf16[1024,256]{1,0:T(8,128)(2,1)} %constant.12.clone.col_hbm, bf16[512,1024]{1,0:T(8,128)(2,1)} %constant.13.clone.row_hbm, bf16[1024,1024]{1,0:T(8,128)(2,1)} %constant.14.clone.embed_hbm, f32[1024,128]{1,0:T(8,128)} %constant.15.clone.scale_hbm), custom_call_target="tpu_custom_call" | custom-call | tf_op jit(solution)/shard_map/exchange/pallas_call | solution.py:256
  30.9 3.9 %images.1 = f32[1,2,256,1024]{3,2,1,0:T(8,128)} custom-call(bf16[256,128]{1,0:T(8,128)(2,1)} %exchange.1.mixture, bf16[128,2048]{1,0:T(8,128)(2,1)} %constant.16.clone.table, f32[1,1024]{1,0:T(1,128)} %constant.17.clone.weight), custom_call_target="tpu_custom_call" | custom-call | tf_op jit(solution)/shard_map/images/pallas_call | solution.py:291

commit v2 on v1

--- a/solution.py
+++ b/solution.py
@@ -17,6 +17,10 @@
 NBLK = 8
 LANES = 2 * CONTRIB
 TAPER_SCALE = 16.0
+LOADS = 4
+SAVES = 4
+JOINT = 4
+ROOM = 24 * 2**20
 MESH = pl.DeviceIdType.MESH
 
 
@@ -72,48 +76,89 @@
 SINE = [(-1.0) ** k * math.pi ** (2 * k) / math.factorial(2 * k + 1) for k in range(7)]
 
 
-def grid_kernel(tiles, coords, values, out, total):
+def grid_kernel(tiles, coords_hbm, values_hbm, out, coords, values, total, load_sem):
     blocks = coords.shape[0]
+    chunk = blocks // LOADS
+
+    def loads(i):
+        part = pl.ds(i * chunk, chunk)
+        return (
+            pltpu.make_async_copy(coords_hbm.at[part], coords.at[part], load_sem.at[i, 0]),
+            pltpu.make_async_copy(values_hbm.at[part], values.at[part], load_sem.at[i, 1]),
+        )
+
+    for i in range(LOADS):
+        for load in loads(i):
+            load.start()
     total[...] = jnp.zeros_like(total)
-    pixel = lax.broadcasted_iota(jnp.int32, (TILE, 1), 0)
-    place = pixel.astype(jnp.float32)
-    flip = 1.0 - 2.0 * (pixel % 2).astype(jnp.float32)
-
-    def block(b, carry):
-        where = coords[b]
+    lane = lax.broadcasted_iota(jnp.int32, (8, 1), 0)
+    step = lane.astype(jnp.float32)
+    flip = 1.0 - 2.0 * (lane % 2).astype(jnp.float32)
+
+    def several(b, carry):
+        where = coords[pl.ds(b * JOINT, JOINT)]
+        count, axes, visible = where.shape
+        where = where.reshape(count * axes, visible)
         nearest = jnp.floor(where + 0.5)
+        where = jnp.where(where == nearest, where * (1.0 + 2.0**-23) + 1e-30, where)
         offset = where - nearest
-        offset = jnp.where(offset == 0.0, 1e-30, offset)
         square = offset * offset
-        wave = jnp.full_like(square, SINE[6])
-        for k in range(5, -1, -1):
+        wave = square * SINE[6] + SINE[5]
+        for k in range(4, -1, -1):
             wave = wave * square + SINE[k]
         half = nearest * 0.5
         odd = (half - jnp.floor(half)) * 4.0 - 1.0
         wave = wave * offset * odd
 
-        def rows(axis):
-            distance = (place - nearest[axis : axis + 1]) - offset[axis : axis + 1]
-            near = pl.reciprocal(distance, approx=True)
-            near = near * (2.0 - distance * near)
-            fall = jnp.exp(distance * distance * (-1.0 / (TAPER_SCALE * TAPER_SCALE)))
-            return (flip * wave[axis : axis + 1]) * fall * near
-
-        along = rows(0).astype(jnp.bfloat16)
-        down = rows(1)
-        data = values[b]
-        right = jnp.concatenate([down * data[0:1], down * data[1:2]], 0).astype(jnp.bfloat16)
-        patch = lax.dot_general(
-            along, right, (((1,), (1,)), ((), ())), preferred_element_type=jnp.float32
-        )
-        tile = tiles[0, b]
-        r = pl.ds(pl.multiple_of(tile // (SUB // TILE) * TILE, TILE), TILE)
-        c = pl.ds(pl.multiple_of(tile % (SUB // TILE) * (2 * TILE), 2 * TILE), 2 * TILE)
-        total[r, c] += patch
+        def rows(i):
+            base = step - where[i : i + 1]
+            fall = jnp.exp(base * base * (-1.0 / (TAPER_SCALE * TAPER_SCALE)))
+            ratio = jnp.exp(base * (-16.0 / (TAPER_SCALE * TAPER_SCALE)))
+            height = (flip * wave[i : i + 1]) * fall
+            result = []
+            for a in range(TILE // 8):
+                distance = base + 8.0 * a if a else base
+                near = pl.reciprocal(distance, approx=True)
+                near = near * (2.0 - distance * near)
+                result.append(height * near)
+                height = height * ratio
+            return jnp.concatenate(result, 0).astype(jnp.bfloat16)
+
+        for i in range(count):
+            along = rows(2 * i)
+            down = rows(2 * i + 1).reshape(TILE // 16, 16, visible)
+            data = values[b * JOINT + i]
+            right = jnp.concatenate(
+                [
+                    (down * jnp.broadcast_to(data[c : c + 1], (16, visible)).astype(jnp.bfloat16))
+                    .reshape(TILE, visible)
+                    for c in range(2)
+                ],
+                0,
+            )
+            patch = lax.dot_general(
+                along, right, (((1,), (1,)), ((), ())), preferred_element_type=jnp.float32
+            )
+            tile = tiles[0, b * JOINT + i]
+            r = pl.ds(pl.multiple_of(tile // (SUB // TILE) * TILE, TILE), TILE)
+            c = pl.ds(pl.multiple_of(tile % (SUB // TILE) * (2 * TILE), 2 * TILE), 2 * TILE)
+            total[r, c] += patch
         return carry
 
-    lax.fori_loop(0, blocks, block, 0, unroll=4)
-    out[...] = total[...].astype(jnp.bfloat16)
+    def portion(i, carry):
+        for load in loads(i):
+            load.wait()
+        return lax.fori_loop(i * (chunk // JOINT), (i + 1) * (chunk // JOINT), several, carry)
+
+    lax.fori_loop(0, LOADS, portion, 0)
+    group = lax.broadcasted_iota(jnp.int32, (TILE, 2 * TILE), 0) // 8
+    other = lax.broadcasted_iota(jnp.int32, (TILE, 2 * TILE), 1) % TILE // 8
+    power = (group * group + other * other).astype(jnp.float32)
+    scale = jnp.exp(power * (-64.0 / (TAPER_SCALE * TAPER_SCALE)))
+    for a in range(SUB // TILE):
+        for e in range(SUB // TILE):
+            part = (slice(a * TILE, (a + 1) * TILE), slice(e * 2 * TILE, (e + 1) * 2 * TILE))
+            out[part] = (total[part] * scale).astype(jnp.bfloat16)
 
 
 def swapped(index, bits):
@@ -153,9 +198,8 @@
     for k in range(1, vis_count):
         pl.semaphore_signal(barrier, inc=1, device_id=(me_g, peers_v[k]), device_id_type=MESH)
 
-    loads[0].wait()
-    loads[1].wait()
-    loads[2].wait()
+    for load in loads[:3]:
+        load.wait()
     for g in range(groups):
         image = jnp.dot(
             part[...], col[:, 2 * LANES * g : 2 * LANES * (g + 1)], preferred_element_type=jnp.float32
@@ -223,9 +267,24 @@
             copy3(k, j).wait_send()
 
 
-def image_kernel(mixture, table, weight, out):
-    result = jnp.dot(mixture[...], table[...], preferred_element_type=jnp.float32)
-    out[0, 0] = result * weight[...]
+def image_kernel(mixture, table, weight, out, image, save_sem):
+    rows_here = mixture.shape[0]
+    saves = []
+    for c in range(2):
+        for h in range(SAVES):
+            part = slice(h * (rows_here // SAVES), (h + 1) * (rows_here // SAVES))
+            result = jnp.dot(
+                mixture[part], table[:, c * FAC : (c + 1) * FAC], preferred_element_type=jnp.float32
+            )
+            image[c, part] = result * weight[...]
+            saves.append(
+                pltpu.make_async_copy(
+                    image.at[c, part], out.at[0, c, part], save_sem.at[c * SAVES + h]
+                )
+            )
+            saves[-1].start()
+    for save in saves:
+        save.wait()
 
 
 def shards(grid_count, vis_count, vis_coords, vis_values, tile_index):
@@ -234,6 +293,9 @@
     rows_here = FAC // vis_count
     unitary = 1.0 / math.sqrt(SUB)
     bf16, f32 = jnp.bfloat16, jnp.float32
+    far = pl.BlockSpec(memory_space=pltpu.HBM)
+    inside = pl.BlockSpec(memory_space=pltpu.VMEM)
+    dma = pltpu.SemaphoreType.DMA
     blocks = vis_coords.shape[1]
     visible = vis_coords.shape[3]
     partial = pl.pallas_call(
@@ -241,22 +303,25 @@
         out_shape=jax.ShapeDtypeStruct((SUB, 2 * SUB), bf16),
         in_specs=[
             pl.BlockSpec(memory_space=pltpu.SMEM),
-            pl.BlockSpec(memory_space=pltpu.VMEM),
-            pl.BlockSpec(memory_space=pltpu.VMEM),
+            far,
+            far,
         ],
         out_specs=pl.BlockSpec(memory_space=pltpu.VMEM),
-        scratch_shapes=[pltpu.VMEM((SUB, 2 * SUB), f32)],
+        scratch_shapes=[
+            pltpu.VMEM((blocks, 2, visible), f32),
+            pltpu.VMEM((blocks, 2, visible), f32),
+            pltpu.VMEM((SUB, 2 * SUB), f32),
+            dma((LOADS, 2)),
+        ],
         name="gridding",
     )(tile_index, vis_coords.reshape(blocks, 2, visible), vis_values.reshape(blocks, 2, visible))
 
     row_scale = taper() * (unitary / math.sqrt(CONTRIB * groups))
     row_scale = np.broadcast_to(row_scale[:, None], (FAC, LANES)).astype(np.float32)
-    any_spec = pl.BlockSpec(memory_space=pl.ANY)
-    dma = pltpu.SemaphoreType.DMA
     mixture = pl.pallas_call(
         functools.partial(exchange_kernel, grid_count, vis_count, unitary),
         out_shape=jax.ShapeDtypeStruct((rows_here, groups * LANES), bf16),
-        in_specs=[any_spec] * 5,
+        in_specs=[far] * 5,
         out_specs=pl.BlockSpec(memory_space=pltpu.VMEM),
         scratch_shapes=[
             pltpu.VMEM((SUB, 2 * SUB), bf16),
@@ -286,18 +351,13 @@
         jnp.asarray(row_scale),
     )
 
-    halves = 2
-    wide = FAC // halves
     return pl.pallas_call(
         image_kernel,
-        grid=(2, halves),
         out_shape=jax.ShapeDtypeStruct((1, 2, rows_here, FAC), f32),
-        in_specs=[
-            pl.BlockSpec((rows_here, groups * LANES), lambda c, h: (0, 0)),
-            pl.BlockSpec((groups * LANES, wide), lambda c, h: (0, c * halves + h)),
-            pl.BlockSpec((1, wide), lambda c, h: (0, h)),
-        ],
-        out_specs=pl.BlockSpec((1, 1, rows_here, wide), lambda c, h: (0, c, 0, h)),
+        in_specs=[inside] * 3,
+        out_specs=far,
+        scratch_shapes=[pltpu.VMEM((2, rows_here, FAC), f32), dma((2 * SAVES,))],
+        compiler_params=pltpu.CompilerParams(vmem_limit_bytes=ROOM),
         name="images",
     )(
         mixture,

time: 35 us -> 31.6 us (0.903)
  Pallas kernels: 34.8 us -> 30.4 us
  local copies, waits for them, and re-layouts: 0 us -> 0.85 us
    pallas_call x1, Pallas kernels: 3.88 us -> 1.57 us  [shards(): pl.pallas_call(image_kernel, out_shape=jax.ShapeDtypeStruct((1, 2, rows_h...]
    pallas_call x1, Pallas kernels: 13 us -> 10.9 us  [shards(): pl.pallas_call(grid_kernel, out_shape=jax.ShapeDtypeStruct((SUB, 2 * SUB)...]
    unnamed x0 -> x6, local copies, waits for them, and re-layouts: none -> 0.85 us
where the time goes in v2:
time: 31.6 us; the launch traced here: 31.3 us
  Pallas kernels  30.4 us (96%)
  local copies, waits for them, and re-layouts  0.85 us (3%)
    pallas_call x1, Pallas kernels, shards(): pl.pallas_call(functools.partial(exchange_kernel, grid_count, vis_count,...  18 us
    pallas_call x1, Pallas kernels, shards(): pl.pallas_call(grid_kernel, out_shape=jax.ShapeDtypeStruct((SUB, 2 * SUB)...  10.9 us
    pallas_call x1, Pallas kernels, shards(): pl.pallas_call(image_kernel, out_shape=jax.ShapeDtypeStruct((1, 2, rows_h...  1.57 us
    unnamed x6, local copies, waits for them, and re-layouts  0.85 us

profile of v2, /device:TPU:0, one launch (start us, length us, event | category | flops | bytes accessed | tf_op | source)
XLA Modules:
  0.0 31.3 jit_solution(7871032052698128992)
XLA Ops:
  0.0 10.9 %gridding.1.part_hbm = bf16[512,1024]{1,0:T(8,128)(2,1)} custom-call(s32[1,64]{1,0:T(1,128)} %tiles.1, f32[64,2,512]{2,1,0:T(2,128)} %bitcast.2, f32[64,2,512]{2,1,0:T(2,128)} %bitcast.3), custom_call_target="tpu_custom_call" | custom-call | tf_op jit(solution)/shard_map/gridding/pallas_call | solution.py:301
  10.9 0.0 copy-start
  10.9 0.0 copy-start.2
  10.9 18.0 %exchange.1.mixture = bf16[256,128]{1,0:T(8,128)(2,1)} custom-call(bf16[512,1024]{1,0:T(8,128)(2,1)} %gridding.1.part_hbm, bf16[1024,256]{1,0:T(8,128)(2,1)} %constant.12.clone.col_hbm, bf16[512,1024]{1,0:T(8,128)(2,1)} %constant.13.clone.row_hbm, bf16[1024,1024]{1,0:T(8,128)(2,1)} %constant.14.clone.embed_hbm, f32[1024,128]{1,0:T(8,128)} %constant.15.clone.scale_hbm), custom_call_target="tpu_custom_call" | custom-call | tf_op jit(solution)/shard_map/exchange/pallas_call | solution.py:321
  28.9 0.0 copy-done
  28.9 0.0 copy-done.2
  28.9 0.0 copy-start.1
  28.9 0.8 %copy-done.1 = bf16[256,128]{1,0:T(8,128)(2,1)S(1)} copy-done((bf16[256,128]{1,0:T(8,128)(2,1)S(1)}, bf16[256,128]{1,0:T(8,128)(2,1)}, u32[]{:S(2)}) %copy-start.1) | copy-done | bytes 65560
  29.8 1.6 %images.1 = f32[1,2,256,1024]{3,2,1,0:T(8,128)} custom-call(bf16[256,128]{1,0:T(8,128)(2,1)S(1)} %copy-done.1, bf16[128,2048]{1,0:T(8,128)(2,1)S(1)} %copy-done, f32[1,1024]{1,0:T(1,128)S(1)} %copy-done.2), custom_call_target="tpu_custom_call" | custom-call | tf_op jit(solution)/shard_map/images/pallas_call | solution.py:354
Async XLA Ops:
  10.9 18.0 %copy-start = (bf16[128,2048]{1,0:T(8,128)(2,1)S(1)}, bf16[128,2048]{1,0:T(8,128)(2,1)}, u32[]{:S(2)}) copy-start(bf16[128,2048]{1,0:T(8,128)(2,1)} %constant.16.clone.table) | copy-start | bytes 1572868
  10.9 18.0 %copy-start.2 = (f32[1,1024]{1,0:T(1,128)S(1)}, f32[1,1024]{1,0:T(1,128)}, u32[]{:S(2)}) copy-start(f32[1,1024]{1,0:T(1,128)} %constant.17.clone.weight) | copy-start | bytes 12292
  28.9 0.8 %copy-start.1 = (bf16[256,128]{1,0:T(8,128)(2,1)S(1)}, bf16[256,128]{1,0:T(8,128)(2,1)}, u32[]{:S(2)}) copy-start(bf16[256,128]{1,0:T(8,128)(2,1)} %exchange.1.mixture) | copy-start | bytes 196612

commit v3 on v2

--- a/solution.py
+++ b/solution.py
@@ -17,9 +17,8 @@
 NBLK = 8
 LANES = 2 * CONTRIB
 TAPER_SCALE = 16.0
-LOADS = 4
 SAVES = 4
-JOINT = 4
+JOINT = 16
 ROOM = 24 * 2**20
 MESH = pl.DeviceIdType.MESH
 
@@ -76,26 +75,32 @@
 SINE = [(-1.0) ** k * math.pi ** (2 * k) / math.factorial(2 * k + 1) for k in range(7)]
 
 
-def grid_kernel(tiles, coords_hbm, values_hbm, out, coords, values, total, load_sem):
+def grid_kernel(
+    tiles_hbm, coords_hbm, values_hbm, out, tiles, coords, values, total, tile_sem, load_sem
+):
     blocks = coords.shape[0]
-    chunk = blocks // LOADS
 
     def loads(i):
-        part = pl.ds(i * chunk, chunk)
+        part = pl.ds(i * JOINT, JOINT)
         return (
             pltpu.make_async_copy(coords_hbm.at[part], coords.at[part], load_sem.at[i, 0]),
             pltpu.make_async_copy(values_hbm.at[part], values.at[part], load_sem.at[i, 1]),
         )
 
-    for i in range(LOADS):
+    for i in range(blocks // JOINT):
         for load in loads(i):
             load.start()
+        if i == 0:
+            tile_load = pltpu.make_async_copy(tiles_hbm, tiles, tile_sem)
+            tile_load.start()
     total[...] = jnp.zeros_like(total)
     lane = lax.broadcasted_iota(jnp.int32, (8, 1), 0)
     step = lane.astype(jnp.float32)
     flip = 1.0 - 2.0 * (lane % 2).astype(jnp.float32)
 
     def several(b, carry):
+        for load in loads(b):
+            load.wait()
         where = coords[pl.ds(b * JOINT, JOINT)]
         count, axes, visible = where.shape
         where = where.reshape(count * axes, visible)
@@ -118,9 +123,7 @@
             result = []
             for a in range(TILE // 8):
                 distance = base + 8.0 * a if a else base
-                near = pl.reciprocal(distance, approx=True)
-                near = near * (2.0 - distance * near)
-                result.append(height * near)
+                result.append(height / distance)
                 height = height * ratio
             return jnp.concatenate(result, 0).astype(jnp.bfloat16)
 
@@ -145,12 +148,8 @@
             total[r, c] += patch
         return carry
 
-    def portion(i, carry):
-        for load in loads(i):
-            load.wait()
-        return lax.fori_loop(i * (chunk // JOINT), (i + 1) * (chunk // JOINT), several, carry)
-
-    lax.fori_loop(0, LOADS, portion, 0)
+    tile_load.wait()
+    lax.fori_loop(0, blocks // JOINT, several, 0)
     group = lax.broadcasted_iota(jnp.int32, (TILE, 2 * TILE), 0) // 8
     other = lax.broadcasted_iota(jnp.int32, (TILE, 2 * TILE), 1) % TILE // 8
     power = (group * group + other * other).astype(jnp.float32)
@@ -172,9 +171,9 @@
 
 
 def exchange_kernel(
-    grid_count, vis_count, unitary, part_hbm, col_hbm, row_hbm, embed_hbm, scale_hbm, out,
-    part, col, row, embed, scale, spectra, pieces, summed, gathered,
-    load_sem, send1, recv1, send2, recv2, send3, recv3,
+    grid_count, vis_count, unitary, part, col, row, embed, scale, out,
+    spectra, pieces, summed, gathered,
+    send1, recv1, send2, recv2, send3, recv3,
 ):
     me_g, me_v = lax.axis_index("grid"), lax.axis_index("vis")
     groups = grid_count // NBLK
@@ -183,23 +182,12 @@
     peers_v = [lax.rem(me_v + k, vis_count) for k in range(vis_count)]
     peers_g = [swapped(me_g, k) for k in range(grid_count)]
     mine = pl.ds(pl.multiple_of(me_v * rows_here, rows_here), rows_here)
-    loads = [
-        pltpu.make_async_copy(src, dst, load_sem.at[i])
-        for i, (src, dst) in enumerate(
-            [(part_hbm, part), (col_hbm, col), (row_hbm, row),
-             (embed_hbm.at[mine], embed), (scale_hbm.at[mine], scale)]
-        )
-    ]
-    for load in loads:
-        load.start()
     barrier = pltpu.get_barrier_semaphore()
     for k in range(grid_count - 1, 0, -1):
         pl.semaphore_signal(barrier, inc=1, device_id=(peers_g[k], me_v), device_id_type=MESH)
     for k in range(1, vis_count):
         pl.semaphore_signal(barrier, inc=1, device_id=(me_g, peers_v[k]), device_id_type=MESH)
 
-    for load in loads[:3]:
-        load.wait()
     for g in range(groups):
         image = jnp.dot(
             part[...], col[:, 2 * LANES * g : 2 * LANES * (g + 1)], preferred_element_type=jnp.float32
@@ -246,8 +234,6 @@
             copy2(k).wait_recv()
         for j in range(1, vis_count):
             copy3(k, j).start()
-    loads[3].wait()
-    loads[4].wait()
     for k in range(grid_count):
         for j in range(1, vis_count):
             copy3(k, j).wait_recv()
@@ -256,8 +242,8 @@
         straight = gathered[NBLK * g : NBLK * (g + 1)].reshape(SUB, LANES)
         turned = pltpu.roll(straight.astype(jnp.float32), CONTRIB, 1) * sign
         both = jnp.concatenate([straight, turned.astype(jnp.bfloat16)], 0)
-        mixture = jnp.dot(embed[...], both, preferred_element_type=jnp.float32)
-        out[:, LANES * g : LANES * (g + 1)] = (mixture * scale[...]).astype(jnp.bfloat16)
+        mixture = jnp.dot(embed[mine], both, preferred_element_type=jnp.float32)
+        out[:, LANES * g : LANES * (g + 1)] = (mixture * scale[mine]).astype(jnp.bfloat16)
     for k in range(1, vis_count):
         copy1(k).wait_send()
     for k in range(1, grid_count):
@@ -302,38 +288,40 @@
         grid_kernel,
         out_shape=jax.ShapeDtypeStruct((SUB, 2 * SUB), bf16),
         in_specs=[
-            pl.BlockSpec(memory_space=pltpu.SMEM),
+            far,
             far,
             far,
         ],
         out_specs=pl.BlockSpec(memory_space=pltpu.VMEM),
         scratch_shapes=[
+            pltpu.SMEM((1, blocks), jnp.int32),
             pltpu.VMEM((blocks, 2, visible), f32),
             pltpu.VMEM((blocks, 2, visible), f32),
             pltpu.VMEM((SUB, 2 * SUB), f32),
-            dma((LOADS, 2)),
+            dma,
+            dma((blocks // JOINT, 2)),
         ],
+        compiler_params=pltpu.CompilerParams(vmem_limit_bytes=ROOM),
+        cost_estimate=pl.CostEstimate(flops=10**10, bytes_accessed=10**6, transcendentals=10**6),
         name="gridding",
-    )(tile_index, vis_coords.reshape(blocks, 2, visible), vis_values.reshape(blocks, 2, visible))
+    )(
+        pltpu.with_memory_space_constraint(tile_index, pltpu.HBM),
+        pltpu.with_memory_space_constraint(vis_coords.reshape(blocks, 2, visible), pltpu.HBM),
+        pltpu.with_memory_space_constraint(vis_values.reshape(blocks, 2, visible), pltpu.HBM),
+    )
 
     row_scale = taper() * (unitary / math.sqrt(CONTRIB * groups))
     row_scale = np.broadcast_to(row_scale[:, None], (FAC, LANES)).astype(np.float32)
     mixture = pl.pallas_call(
         functools.partial(exchange_kernel, grid_count, vis_count, unitary),
         out_shape=jax.ShapeDtypeStruct((rows_here, groups * LANES), bf16),
-        in_specs=[far] * 5,
+        in_specs=[inside] * 5,
         out_specs=pl.BlockSpec(memory_space=pltpu.VMEM),
         scratch_shapes=[
-            pltpu.VMEM((SUB, 2 * SUB), bf16),
-            pltpu.VMEM((2 * SUB, groups * 2 * LANES), bf16),
-            pltpu.VMEM((SUB, 2 * SUB), bf16),
-            pltpu.VMEM((rows_here, 2 * SUB), bf16),
-            pltpu.VMEM((rows_here, LANES), f32),
             pltpu.VMEM((vis_count, grid_count, quarter, LANES), bf16),
             pltpu.VMEM((vis_count, grid_count, quarter, LANES), bf16),
             pltpu.VMEM((grid_count, quarter, LANES), bf16),
             pltpu.VMEM((grid_count, vis_count, quarter, LANES), bf16),
-            dma((5,)),
             dma((vis_count,)),
             dma((vis_count,)),
             dma((grid_count,)),
@@ -341,7 +329,10 @@
             dma((grid_count, vis_count)),
             dma((grid_count, vis_count)),
         ],
-        compiler_params=pltpu.CompilerParams(collective_id=0, has_side_effects=True),
+        compiler_params=pltpu.CompilerParams(
+            collective_id=0, has_side_effects=True, vmem_limit_bytes=ROOM
+        ),
+        cost_estimate=pl.CostEstimate(flops=10**10, bytes_accessed=10**6, transcendentals=0),
         name="exchange",
     )(
         partial,

time: 31.6 us -> 24 us (0.76)
  Pallas kernels: 30.4 us -> 23.7 us
  local copies, waits for them, and re-layouts: 0.85 us -> 0.03 us
    pallas_call x1, Pallas kernels: 10.9 us -> 6.14 us  [shards(): pl.pallas_call(grid_kernel, out_shape=jax.ShapeDtypeStruct((SUB, 2 * SUB)...]
    pallas_call x1, Pallas kernels: 18 us -> 16 us  [shards(): pl.pallas_call(functools.partial(exchange_kernel, grid_count, vis_count,...]
    unnamed x6 -> x12, local copies, waits for them, and re-layouts: 0.85 us -> 0.03 us
where the time goes in v3:
time: 24 us; the launch traced here: 23.8 us
  Pallas kernels  23.7 us (99%)
    pallas_call x1, Pallas kernels, shards(): pl.pallas_call(functools.partial(exchange_kernel, grid_count, vis_count,...  16 us
    pallas_call x1, Pallas kernels, shards(): pl.pallas_call(grid_kernel, out_shape=jax.ShapeDtypeStruct((SUB, 2 * SUB)...  6.14 us
    pallas_call x1, Pallas kernels, shards(): pl.pallas_call(image_kernel, out_shape=jax.ShapeDtypeStruct((1, 2, rows_h...  1.57 us

profile of v3, /device:TPU:0, one launch (start us, length us, event | category | flops | bytes accessed | tf_op | source)
XLA Modules:
  0.0 23.8 jit_solution(3736596624754747201)
XLA Ops:
  0.0 0.0 copy-start.2
  0.0 0.0 copy-start.3
  0.0 0.0 copy-start.4
  0.0 0.0 copy-start.5
  0.0 6.1 %gridding.1.part = bf16[512,1024]{1,0:T(8,128)(2,1)S(1)} custom-call(s32[1,64]{1,0:T(1,128)} %tiles_hbm.1, f32[64,2,512]{2,1,0:T(2,128)} %bitcast.2, f32[64,2,512]{2,1,0:T(2,128)} %bitcast.3), custom_call_target="tpu_custom_call" | custom-call | flops 10000000000 | bytes 1000000 | tf_op jit(solution)/shard_map/gridding/pallas_call | solution.py:287
  6.2 0.0 copy-done.2
  6.2 0.0 copy-done.3
  6.2 0.0 copy-done.4
  6.2 0.0 copy-done.5
  6.2 0.0 copy-start
  6.2 0.0 copy-start.1
  6.2 16.0 %exchange.1.mixture = bf16[256,128]{1,0:T(8,128)(2,1)S(1)} custom-call(bf16[512,1024]{1,0:T(8,128)(2,1)S(1)} %gridding.1.part, bf16[1024,256]{1,0:T(8,128)(2,1)S(1)} %copy-done.5, bf16[512,1024]{1,0:T(8,128)(2,1)S(1)} %copy-done.3, bf16[1024,1024]{1,0:T(8,128)(2,1)S(1)} %copy-done.2, f32[1024,128]{1,0:T(8,128)S(1)} %copy-done.4), custom_call_target="tpu_custom_call" | custom-call | flops 10000000000 | bytes 1000000 | tf_op jit(solution)/shard_map/exchange/pallas_call | solution.py:315
  22.2 0.0 copy-done
  22.2 0.0 copy-done.1
  22.2 1.6 %images.1 = f32[1,2,256,1024]{3,2,1,0:T(8,128)} custom-call(bf16[256,128]{1,0:T(8,128)(2,1)S(1)} %exchange.1.mixture, bf16[128,2048]{1,0:T(8,128)(2,1)S(1)} %copy-done, f32[1,1024]{1,0:T(1,128)S(1)} %copy-done.1), custom_call_target="tpu_custom_call" | custom-call | tf_op jit(solution)/shard_map/images/pallas_call | solution.py:345
Async XLA Ops:
  0.0 6.2 %copy-start.2 = (bf16[1024,1024]{1,0:T(8,128)(2,1)S(1)}, bf16[1024,1024]{1,0:T(8,128)(2,1)}, u32[]{:S(2)}) copy-start(bf16[1024,1024]{1,0:T(8,128)(2,1)} %constant.14.clone.embed) | copy-start | bytes 6291460
  0.0 6.2 %copy-start.3 = (bf16[512,1024]{1,0:T(8,128)(2,1)S(1)}, bf16[512,1024]{1,0:T(8,128)(2,1)}, u32[]{:S(2)}) copy-start(bf16[512,1024]{1,0:T(8,128)(2,1)} %constant.13.clone.row) | copy-start | bytes 3145732
  0.0 6.2 %copy-start.4 = (f32[1024,128]{1,0:T(8,128)S(1)}, f32[1024,128]{1,0:T(8,128)}, u32[]{:S(2)}) copy-start(f32[1024,128]{1,0:T(8,128)} %constant.15.clone.scale) | copy-start | bytes 1572868
  0.0 6.2 %copy-start.5 = (bf16[1024,256]{1,0:T(8,128)(2,1)S(1)}, bf16[1024,256]{1,0:T(8,128)(2,1)}, u32[]{:S(2)}) copy-start(bf16[1024,256]{1,0:T(8,128)(2,1)} %constant.12.clone.col) | copy-start | bytes 1572868
  6.2 16.0 %copy-start = (bf16[128,2048]{1,0:T(8,128)(2,1)S(1)}, bf16[128,2048]{1,0:T(8,128)(2,1)}, u32[]{:S(2)}) copy-start(bf16[128,2048]{1,0:T(8,128)(2,1)} %constant.16.clone.table) | copy-start | bytes 1572868
  6.2 16.0 %copy-start.1 = (f32[1,1024]{1,0:T(1,128)S(1)}, f32[1,1024]{1,0:T(1,128)}, u32[]{:S(2)}) copy-start(f32[1,1024]{1,0:T(1,128)} %constant.17.clone.weight) | copy-start | bytes 12292

commit v4 on v3

--- a/solution.py
+++ b/solution.py
@@ -76,7 +76,7 @@
 
 
 def grid_kernel(
-    tiles_hbm, coords_hbm, values_hbm, out, tiles, coords, values, total, tile_sem, load_sem
+    tiles_hbm, coords_hbm, values_hbm, total, tiles, coords, values, tile_sem, load_sem
 ):
     blocks = coords.shape[0]
 
@@ -150,14 +150,6 @@
 
     tile_load.wait()
     lax.fori_loop(0, blocks // JOINT, several, 0)
-    group = lax.broadcasted_iota(jnp.int32, (TILE, 2 * TILE), 0) // 8
-    other = lax.broadcasted_iota(jnp.int32, (TILE, 2 * TILE), 1) % TILE // 8
-    power = (group * group + other * other).astype(jnp.float32)
-    scale = jnp.exp(power * (-64.0 / (TAPER_SCALE * TAPER_SCALE)))
-    for a in range(SUB // TILE):
-        for e in range(SUB // TILE):
-            part = (slice(a * TILE, (a + 1) * TILE), slice(e * 2 * TILE, (e + 1) * 2 * TILE))
-            out[part] = (total[part] * scale).astype(jnp.bfloat16)
 
 
 def swapped(index, bits):
@@ -171,8 +163,8 @@
 
 
 def exchange_kernel(
-    grid_count, vis_count, unitary, part, col, row, embed, scale, out,
-    spectra, pieces, summed, gathered,
+    grid_count, vis_count, unitary, total, col, row, embed, scale, out,
+    part, spectra, pieces, summed, gathered,
     send1, recv1, send2, recv2, send3, recv3,
 ):
     me_g, me_v = lax.axis_index("grid"), lax.axis_index("vis")
@@ -188,6 +180,14 @@
     for k in range(1, vis_count):
         pl.semaphore_signal(barrier, inc=1, device_id=(me_g, peers_v[k]), device_id_type=MESH)
 
+    group = lax.broadcasted_iota(jnp.int32, (TILE, 2 * TILE), 0) // 8
+    other = lax.broadcasted_iota(jnp.int32, (TILE, 2 * TILE), 1) % TILE // 8
+    power = (group * group + other * other).astype(jnp.float32)
+    fall = jnp.exp(power * (-64.0 / (TAPER_SCALE * TAPER_SCALE)))
+    for a in range(SUB // TILE):
+        for e in range(SUB // TILE):
+            spot = (slice(a * TILE, (a + 1) * TILE), slice(e * 2 * TILE, (e + 1) * 2 * TILE))
+            part[spot] = (total[spot] * fall).astype(jnp.bfloat16)
     for g in range(groups):
         image = jnp.dot(
             part[...], col[:, 2 * LANES * g : 2 * LANES * (g + 1)], preferred_element_type=jnp.float32
@@ -200,10 +200,14 @@
 
     pl.semaphore_wait(barrier, grid_count + vis_count - 2)
 
-    def copy1(k):
+    half = grid_count // 2
+    high = me_g // half
+    spots = [pl.ds((1 - high) * half, half), pl.ds(high * half, half)]
+
+    def copy1(h, k):
         return pltpu.make_async_remote_copy(
-            src_ref=spectra.at[peers_v[k]], dst_ref=pieces.at[k], send_sem=send1.at[k],
-            recv_sem=recv1.at[k], device_id=(me_g, peers_v[k]), device_id_type=MESH,
+            src_ref=spectra.at[peers_v[k], spots[h]], dst_ref=pieces.at[k, spots[h]],
+            send_sem=send1.at[h, k], recv_sem=recv1.at[h, k], device_id=(me_g, peers_v[k]), device_id_type=MESH,
         )
 
     def copy2(k):
@@ -219,15 +223,17 @@
             recv_sem=recv3.at[k, j], device_id=(me_g, peers_v[j]), device_id_type=MESH,
         )
 
-    for k in range(1, vis_count):
-        copy1(k).start()
-    whole = spectra[me_v].astype(jnp.float32)
-    for k in range(1, vis_count):
-        copy1(k).wait_recv()
-        whole = whole + pieces[k].astype(jnp.float32)
-    summed[...] = whole.astype(jnp.bfloat16)
-    for k in range(grid_count - 1, 0, -1):
-        copy2(k).start()
+    for h in range(2):
+        for k in range(1, vis_count):
+            copy1(h, k).start()
+    for h in range(2):
+        whole = spectra[me_v, spots[h]].astype(jnp.float32)
+        for k in range(1, vis_count):
+            copy1(h, k).wait_recv()
+            whole = whole + pieces[k, spots[h]].astype(jnp.float32)
+        summed[spots[h]] = whole.astype(jnp.bfloat16)
+        for k in range(grid_count - 1, half - 1, -1) if h == 0 else range(half - 1, 0, -1):
+            copy2(k).start()
     gathered[me_g, me_v] = summed[me_g]
     for k in range(grid_count):
         if k > 0:
@@ -244,8 +250,9 @@
         both = jnp.concatenate([straight, turned.astype(jnp.bfloat16)], 0)
         mixture = jnp.dot(embed[mine], both, preferred_element_type=jnp.float32)
         out[:, LANES * g : LANES * (g + 1)] = (mixture * scale[mine]).astype(jnp.bfloat16)
-    for k in range(1, vis_count):
-        copy1(k).wait_send()
+    for h in range(2):
+        for k in range(1, vis_count):
+            copy1(h, k).wait_send()
     for k in range(1, grid_count):
         copy2(k).wait_send()
     for k in range(grid_count):
@@ -286,7 +293,7 @@
     visible = vis_coords.shape[3]
     partial = pl.pallas_call(
         grid_kernel,
-        out_shape=jax.ShapeDtypeStruct((SUB, 2 * SUB), bf16),
+        out_shape=jax.ShapeDtypeStruct((SUB, 2 * SUB), f32),
         in_specs=[
             far,
             far,
@@ -297,7 +304,6 @@
             pltpu.SMEM((1, blocks), jnp.int32),
             pltpu.VMEM((blocks, 2, visible), f32),
             pltpu.VMEM((blocks, 2, visible), f32),
-            pltpu.VMEM((SUB, 2 * SUB), f32),
             dma,
             dma((blocks // JOINT, 2)),
         ],
@@ -318,12 +324,13 @@
         in_specs=[inside] * 5,
         out_specs=pl.BlockSpec(memory_space=pltpu.VMEM),
         scratch_shapes=[
+            pltpu.VMEM((SUB, 2 * SUB), bf16),
             pltpu.VMEM((vis_count, grid_count, quarter, LANES), bf16),
             pltpu.VMEM((vis_count, grid_count, quarter, LANES), bf16),
             pltpu.VMEM((grid_count, quarter, LANES), bf16),
             pltpu.VMEM((grid_count, vis_count, quarter, LANES), bf16),
-            dma((vis_count,)),
-            dma((vis_count,)),
+            dma((2, vis_count)),
+            dma((2, vis_count)),
             dma((grid_count,)),
             dma((grid_count,)),
             dma((grid_count, vis_count)),

time: 24 us -> 23.7 us (0.987)
  Pallas kernels: 23.7 us -> 23.4 us
where the time goes in v4:
time: 23.7 us; the launch traced here: 23.6 us
  Pallas kernels  23.4 us (99%)
    pallas_call x1, Pallas kernels, shards(): pl.pallas_call(functools.partial(exchange_kernel, grid_count, vis_count,...  15.9 us
    pallas_call x1, Pallas kernels, shards(): pl.pallas_call(grid_kernel, out_shape=jax.ShapeDtypeStruct((SUB, 2 * SUB)...  6 us
    pallas_call x1, Pallas kernels, shards(): pl.pallas_call(image_kernel, out_shape=jax.ShapeDtypeStruct((1, 2, rows_h...  1.57 us

profile of v4, /device:TPU:0, one launch (start us, length us, event | category | flops | bytes accessed | tf_op | source)
XLA Modules:
  0.0 23.6 jit_solution(14414527249071553311)
XLA Ops:
  0.0 0.0 copy-start.2
  0.0 0.0 copy-start.3
  0.0 0.0 copy-start.4
  0.0 0.0 copy-start.5
  0.0 6.0 %gridding.1.total = f32[512,1024]{1,0:T(8,128)S(1)} custom-call(s32[1,64]{1,0:T(1,128)} %tiles_hbm.1, f32[64,2,512]{2,1,0:T(2,128)} %bitcast.2, f32[64,2,512]{2,1,0:T(2,128)} %bitcast.3), custom_call_target="tpu_custom_call" | custom-call | flops 10000000000 | bytes 1000000 | tf_op jit(solution)/shard_map/gridding/pallas_call | solution.py:294
  6.0 0.0 copy-done.2
  6.0 0.0 copy-done.3
  6.0 0.0 copy-done.4
  6.1 0.0 copy-done.5
  6.1 0.0 copy-start
  6.1 0.0 copy-start.1
  6.1 15.9 %exchange.1.mixture = bf16[256,128]{1,0:T(8,128)(2,1)S(1)} custom-call(f32[512,1024]{1,0:T(8,128)S(1)} %gridding.1.total, bf16[1024,256]{1,0:T(8,128)(2,1)S(1)} %copy-done.5, bf16[512,1024]{1,0:T(8,128)(2,1)S(1)} %copy-done.3, bf16[1024,1024]{1,0:T(8,128)(2,1)S(1)} %copy-done.2, f32[1024,128]{1,0:T(8,128)S(1)} %copy-done.4), custom_call_target="tpu_custom_call" | custom-call | flops 10000000000 | bytes 1000000 | tf_op jit(solution)/shard_map/exchange/pallas_call | solution.py:321
  22.0 0.0 copy-done
  22.0 0.0 copy-done.1
  22.0 1.6 %images.1 = f32[1,2,256,1024]{3,2,1,0:T(8,128)} custom-call(bf16[256,128]{1,0:T(8,128)(2,1)S(1)} %exchange.1.mixture, bf16[128,2048]{1,0:T(8,128)(2,1)S(1)} %copy-done, f32[1,1024]{1,0:T(1,128)S(1)} %copy-done.1), custom_call_target="tpu_custom_call" | custom-call | tf_op jit(solution)/shard_map/images/pallas_call | solution.py:352
Async XLA Ops:
  0.0 6.0 %copy-start.2 = (bf16[1024,1024]{1,0:T(8,128)(2,1)S(1)}, bf16[1024,1024]{1,0:T(8,128)(2,1)}, u32[]{:S(2)}) copy-start(bf16[1024,1024]{1,0:T(8,128)(2,1)} %constant.14.clone.embed) | copy-start | bytes 6291460
  0.0 6.0 %copy-start.3 = (bf16[512,1024]{1,0:T(8,128)(2,1)S(1)}, bf16[512,1024]{1,0:T(8,128)(2,1)}, u32[]{:S(2)}) copy-start(bf16[512,1024]{1,0:T(8,128)(2,1)} %constant.13.clone.row) | copy-start | bytes 3145732
  0.0 6.0 %copy-start.4 = (f32[1024,128]{1,0:T(8,128)S(1)}, f32[1024,128]{1,0:T(8,128)}, u32[]{:S(2)}) copy-start(f32[1024,128]{1,0:T(8,128)} %constant.15.clone.scale) | copy-start | bytes 1572868
  0.0 6.0 %copy-start.5 = (bf16[1024,256]{1,0:T(8,128)(2,1)S(1)}, bf16[1024,256]{1,0:T(8,128)(2,1)}, u32[]{:S(2)}) copy-start(bf16[1024,256]{1,0:T(8,128)(2,1)} %constant.12.clone.col) | copy-start | bytes 1572868
  6.1 15.9 %copy-start = (bf16[128,2048]{1,0:T(8,128)(2,1)S(1)}, bf16[128,2048]{1,0:T(8,128)(2,1)}, u32[]{:S(2)}) copy-start(bf16[128,2048]{1,0:T(8,128)(2,1)} %constant.16.clone.table) | copy-start | bytes 1572868
  6.1 15.9 %copy-start.1 = (f32[1,1024]{1,0:T(1,128)S(1)}, f32[1,1024]{1,0:T(1,128)}, u32[]{:S(2)}) copy-start(f32[1,1024]{1,0:T(1,128)} %constant.17.clone.weight) | copy-start | bytes 12292

commit v5 on v4

--- a/solution.py
+++ b/solution.py
@@ -18,7 +18,8 @@
 LANES = 2 * CONTRIB
 TAPER_SCALE = 16.0
 SAVES = 4
-JOINT = 16
+JOINT = 32
+PIECES = 4
 ROOM = 24 * 2**20
 MESH = pl.DeviceIdType.MESH
 
@@ -97,6 +98,7 @@
     lane = lax.broadcasted_iota(jnp.int32, (8, 1), 0)
     step = lane.astype(jnp.float32)
     flip = 1.0 - 2.0 * (lane % 2).astype(jnp.float32)
+    lean = jnp.exp(step * (-16.0 / (TAPER_SCALE * TAPER_SCALE)))
 
     def several(b, carry):
         for load in loads(b):
@@ -114,11 +116,12 @@
         half = nearest * 0.5
         odd = (half - jnp.floor(half)) * 4.0 - 1.0
         wave = wave * offset * odd
+        growth = jnp.exp(where * (16.0 / (TAPER_SCALE * TAPER_SCALE)))
 
         def rows(i):
             base = step - where[i : i + 1]
             fall = jnp.exp(base * base * (-1.0 / (TAPER_SCALE * TAPER_SCALE)))
-            ratio = jnp.exp(base * (-16.0 / (TAPER_SCALE * TAPER_SCALE)))
+            ratio = lean * growth[i : i + 1]
             height = (flip * wave[i : i + 1]) * fall
             result = []
             for a in range(TILE // 8):
@@ -200,9 +203,8 @@
 
     pl.semaphore_wait(barrier, grid_count + vis_count - 2)
 
-    half = grid_count // 2
-    high = me_g // half
-    spots = [pl.ds((1 - high) * half, half), pl.ds(high * half, half)]
+    size = grid_count // PIECES
+    spots = [pl.ds(swapped(me_g // size, h) * size, size) for h in range(PIECES)]
 
     def copy1(h, k):
         return pltpu.make_async_remote_copy(
@@ -223,16 +225,16 @@
             recv_sem=recv3.at[k, j], device_id=(me_g, peers_v[j]), device_id_type=MESH,
         )
 
-    for h in range(2):
+    for h in range(PIECES - 1, -1, -1):
         for k in range(1, vis_count):
             copy1(h, k).start()
-    for h in range(2):
+    for h in range(PIECES - 1, -1, -1):
         whole = spectra[me_v, spots[h]].astype(jnp.float32)
         for k in range(1, vis_count):
             copy1(h, k).wait_recv()
             whole = whole + pieces[k, spots[h]].astype(jnp.float32)
         summed[spots[h]] = whole.astype(jnp.bfloat16)
-        for k in range(grid_count - 1, half - 1, -1) if h == 0 else range(half - 1, 0, -1):
+        for k in range((h + 1) * size - 1, max(h * size - 1, 0), -1):
             copy2(k).start()
     gathered[me_g, me_v] = summed[me_g]
     for k in range(grid_count):
@@ -250,7 +252,7 @@
         both = jnp.concatenate([straight, turned.astype(jnp.bfloat16)], 0)
         mixture = jnp.dot(embed[mine], both, preferred_element_type=jnp.float32)
         out[:, LANES * g : LANES * (g + 1)] = (mixture * scale[mine]).astype(jnp.bfloat16)
-    for h in range(2):
+    for h in range(PIECES):
         for k in range(1, vis_count):
             copy1(h, k).wait_send()
     for k in range(1, grid_count):
@@ -329,8 +331,8 @@
             pltpu.VMEM((vis_count, grid_count, quarter, LANES), bf16),
             pltpu.VMEM((grid_count, quarter, LANES), bf16),
             pltpu.VMEM((grid_count, vis_count, quarter, LANES), bf16),
-            dma((2, vis_count)),
-            dma((2, vis_count)),
+            dma((PIECES, vis_count)),
+            dma((PIECES, vis_count)),
             dma((grid_count,)),
             dma((grid_count,)),
             dma((grid_count, vis_count)),

time: 23.7 us -> 23.5 us (level)
  no operation moved by 1% of the time
where the time goes in v5:
time: 23.5 us; the launch traced here: 23.4 us
  Pallas kernels  23.3 us (99%)
    pallas_call x1, Pallas kernels, shards(): pl.pallas_call(functools.partial(exchange_kernel, grid_count, vis_count,...  15.9 us
    pallas_call x1, Pallas kernels, shards(): pl.pallas_call(grid_kernel, out_shape=jax.ShapeDtypeStruct((SUB, 2 * SUB)...  5.79 us
    pallas_call x1, Pallas kernels, shards(): pl.pallas_call(image_kernel, out_shape=jax.ShapeDtypeStruct((1, 2, rows_h...  1.58 us

profile of v5, /device:TPU:0, one launch (start us, length us, event | category | flops | bytes accessed | tf_op | source)
XLA Modules:
  0.0 23.4 jit_solution(4661870098105072395)
XLA Ops:
  0.0 0.0 copy-start.2
  0.0 0.0 copy-start.3
  0.0 0.0 copy-start.4
  0.0 0.0 copy-start.5
  0.0 5.8 %gridding.1.total = f32[512,1024]{1,0:T(8,128)S(1)} custom-call(s32[1,64]{1,0:T(1,128)} %tiles_hbm.1, f32[64,2,512]{2,1,0:T(2,128)} %bitcast.2, f32[64,2,512]{2,1,0:T(2,128)} %bitcast.3), custom_call_target="tpu_custom_call" | custom-call | flops 10000000000 | bytes 1000000 | tf_op jit(solution)/shard_map/gridding/pallas_call | solution.py:296
  5.8 0.0 copy-done.2
  5.8 0.0 copy-done.3
  5.8 0.0 copy-done.4
  5.8 0.0 copy-done.5
  5.8 0.0 copy-start
  5.9 0.0 copy-start.1
  5.9 15.9 %exchange.1.mixture = bf16[256,128]{1,0:T(8,128)(2,1)S(1)} custom-call(f32[512,1024]{1,0:T(8,128)S(1)} %gridding.1.total, bf16[1024,256]{1,0:T(8,128)(2,1)S(1)} %copy-done.5, bf16[512,1024]{1,0:T(8,128)(2,1)S(1)} %copy-done.3, bf16[1024,1024]{1,0:T(8,128)(2,1)S(1)} %copy-done.2, f32[1024,128]{1,0:T(8,128)S(1)} %copy-done.4), custom_call_target="tpu_custom_call" | custom-call | flops 10000000000 | bytes 1000000 | tf_op jit(solution)/shard_map/exchange/pallas_call | solution.py:323
  21.8 0.0 copy-done
  21.8 0.0 copy-done.1
  21.8 1.6 %images.1 = f32[1,2,256,1024]{3,2,1,0:T(8,128)} custom-call(bf16[256,128]{1,0:T(8,128)(2,1)S(1)} %exchange.1.mixture, bf16[128,2048]{1,0:T(8,128)(2,1)S(1)} %copy-done, f32[1,1024]{1,0:T(1,128)S(1)} %copy-done.1), custom_call_target="tpu_custom_call" | custom-call | tf_op jit(solution)/shard_map/images/pallas_call | solution.py:354
Async XLA Ops:
  0.0 5.8 %copy-start.2 = (bf16[1024,1024]{1,0:T(8,128)(2,1)S(1)}, bf16[1024,1024]{1,0:T(8,128)(2,1)}, u32[]{:S(2)}) copy-start(bf16[1024,1024]{1,0:T(8,128)(2,1)} %constant.14.clone.embed) | copy-start | bytes 6291460
  0.0 5.8 %copy-start.3 = (bf16[512,1024]{1,0:T(8,128)(2,1)S(1)}, bf16[512,1024]{1,0:T(8,128)(2,1)}, u32[]{:S(2)}) copy-start(bf16[512,1024]{1,0:T(8,128)(2,1)} %constant.13.clone.row) | copy-start | bytes 3145732
  0.0 5.8 %copy-start.4 = (f32[1024,128]{1,0:T(8,128)S(1)}, f32[1024,128]{1,0:T(8,128)}, u32[]{:S(2)}) copy-start(f32[1024,128]{1,0:T(8,128)} %constant.15.clone.scale) | copy-start | bytes 1572868
  0.0 5.8 %copy-start.5 = (bf16[1024,256]{1,0:T(8,128)(2,1)S(1)}, bf16[1024,256]{1,0:T(8,128)(2,1)}, u32[]{:S(2)}) copy-start(bf16[1024,256]{1,0:T(8,128)(2,1)} %constant.12.clone.col) | copy-start | bytes 1572868
  5.8 16.0 %copy-start = (bf16[128,2048]{1,0:T(8,128)(2,1)S(1)}, bf16[128,2048]{1,0:T(8,128)(2,1)}, u32[]{:S(2)}) copy-start(bf16[128,2048]{1,0:T(8,128)(2,1)} %constant.16.clone.table) | copy-start | bytes 1572868
  5.9 16.0 %copy-start.1 = (f32[1,1024]{1,0:T(1,128)S(1)}, f32[1,1024]{1,0:T(1,128)}, u32[]{:S(2)}) copy-start(f32[1,1024]{1,0:T(1,128)} %constant.17.clone.weight) | copy-start | bytes 12292
